TPU v7x, 32 devices: a whole 2x2x4 slice. The times are simulated.
32 devices in a mesh: seq: 8 (over y, x, core), mp: 4 (over z).
Axes of the slice: x: 2, y: 2, z: 4, core: 2. Of those that a mesh axis runs over, the one named last changes fastest.
Arguments:
- stream: float32 [4096, 2048], P('seq', 'mp'), may hold values from -6 to 6
- doc_starts: int32 [4096], P('seq'), may hold values 0 or 1
- gain_first: float32 [2048], replicated, may hold values from 0.5 to 1.5
- proj_inner: bfloat16 [2048, 2560], P(None, 'mp'), may hold values from -0.125 to 0.125
- proj_gate: bfloat16 [2048, 2560], P(None, 'mp'), may hold values from -0.125 to 0.125
- conv_weight: float32 [4, 2560], P(None, 'mp'), may hold values from -3 to 3
- conv_bias: float32 [2560], P('mp'), may hold values from -3 to 3
- gate_recur: bfloat16 [16, 160, 160], P('mp'), may hold values from -0.5 to 0.5
- gate_input: bfloat16 [16, 160, 160], P('mp'), may hold values from -0.5 to 0.5
- bias_recur: float32 [2560], P('mp'), may hold values from -3 to 3
- bias_input: float32 [2560], P('mp'), may hold values from -3 to 3
- decay_param: float32 [2560], P('mp'), may hold values from 3.4 to 15, as said below
- proj_out: bfloat16 [2560, 2048], P('mp'), may hold values from -0.25 to 0.25
- gain_second: float32 [2048], replicated, may hold values from 0.5 to 1.5
- mlp_gate: bfloat16 [2048, 6144], P(None, 'mp'), may hold values from -0.125 to 0.125
- mlp_up: bfloat16 [2048, 6144], P(None, 'mp'), may hold values from -0.125 to 0.125
- mlp_down: bfloat16 [6144, 2048], P('mp'), may hold values from -0.15625 to 0.15625
- cotangent: float32 [4096, 2048], P('seq', 'mp'), may hold values from -6 to 6
Outputs:
- output: float32 [4096, 2048], P('seq', 'mp')
- grad_stream: float32 [4096, 2048], P('seq', 'mp')
- grad_gain_first: float32 [2048], replicated
- grad_proj_inner: float32 [2048, 2560], P('seq', 'mp')
- grad_proj_gate: float32 [2048, 2560], P('seq', 'mp')
- grad_conv_weight: float32 [4, 2560], P(None, 'mp')
- grad_conv_bias: float32 [2560], P('mp')
- grad_gate_recur: float32 [16, 160, 160], P('mp')
- grad_gate_input: float32 [16, 160, 160], P('mp')
- grad_bias_recur: float32 [2560], P('mp')
- grad_bias_input: float32 [2560], P('mp')
- grad_decay: float32 [2560], P('mp')
- grad_proj_out: float32 [2560, 2048], P(('mp', 'seq'))
- grad_gain_second: float32 [2048], replicated
- grad_mlp_gate: float32 [2048, 6144], P('seq', 'mp')
- grad_mlp_up: float32 [2048, 6144], P('seq', 'mp')
- grad_mlp_down: float32 [6144, 2048], P(('mp', 'seq'))
Inputs may be any that keep to these rules, and one draw needn't show every extreme that they name: decay_param is -log(exp(q) - 1) for a per-channel rate q between 0.05 / 4096 and 0.03. `doc_starts`: a 1 marks the first token of a document.
All inputs are finite; a program needn't handle non-finite values. No bound on the sum of `doc_starts` on one device may be relied on, other than what follows from the above.
Results may differ from a plain program's by a relative error of at most 0.0089.
Values sent between devices are 32-bit elements; how exact they have to be, the bound alone decides.
No kernel may reach another device: no remote copies, remote signals or barrier semaphores. Data moves between devices by JAX's collectives and lax.ppermute only.
A program may use at most 256 MiB of HBM per device.

v0:
```python
from functools import partial
import jax
import jax.numpy as jnp
from jax import lax
from jax.sharding import PartitionSpec as P

recur_scale = 8.0
norm_eps = 1e-06


def passed_along(value, axis, steps):
    count = lax.axis_size(axis)
    first, last = (max(0, -steps), min(count, count - steps))
    return lax.ppermute(value, axis, [(source, source + steps) for source in range(first, last)])


def carried_in(value, axis, join, neutral, backward):
    count, mine = (lax.axis_size(axis), lax.axis_index(axis))
    pieces = jax.tree.map(lambda part: lax.all_gather(part, axis), value)
    if backward:
        pieces = jax.tree.map(lambda part: part[::-1], pieces)
        mine = count - 1 - mine
    running = jax.tree.map(
        lambda part, zero: jnp.full_like(part, 0) + jnp.asarray(zero, part.dtype), value, neutral
    )

    def turn(position, running):
        longer = join(running, jax.tree.map(lambda part: part[position], pieces))
        return jax.tree.map(lambda new, old: jnp.where(position < mine, new, old), longer, running)

    return lax.fori_loop(0, count - 1, turn, running)


def norm_rows(rows, gain):
    return rows * lax.rsqrt(jnp.mean(rows * rows, axis=-1, keepdims=True) + norm_eps) * gain


def matmul(left, right):
    return jnp.dot(left, right, preferred_element_type=jnp.float32)


def matmul_nt(left, right):
    return lax.dot_general(
        left, right, (((1,), (1,)), ((), ())), preferred_element_type=jnp.float32
    )


def matmul_tn(left, right):
    return lax.dot_general(
        left, right, (((0,), (0,)), ((), ())), preferred_element_type=jnp.float32
    )


def block_apply(values, weights):
    count = values.shape[0]
    groups = weights.shape[0]
    width = weights.shape[1]
    split = values.reshape(count, groups, width)
    mixed = jnp.einsum("tbi,bio->tbo", split, weights, preferred_element_type=jnp.float32)
    return mixed.reshape(count, groups * width)


def block_back(grads, weights):
    count = grads.shape[0]
    groups = weights.shape[0]
    width = weights.shape[1]
    split = grads.reshape(count, groups, width)
    mixed = jnp.einsum("tbo,bio->tbi", split, weights, preferred_element_type=jnp.float32)
    return mixed.reshape(count, groups * width)


def block_grad(values, grads, groups):
    count = values.shape[0]
    width = values.shape[1] // groups
    left = values.reshape(count, groups, width)
    right = grads.reshape(count, groups, width)
    return jnp.einsum("tbi,tbo->bio", left, right, preferred_element_type=jnp.float32)


def link(earlier, later):
    return (later[0] * earlier[0], later[0] * earlier[1] + later[1])


def local_scan(starts, conv_out, recur_pre, input_pre, decay):
    recur = jax.nn.sigmoid(recur_pre)
    entry = jax.nn.sigmoid(input_pre)
    log_decay = -recur_scale * recur * jax.nn.softplus(-decay)
    factor = starts + (1.0 - starts) * jnp.sqrt(-jnp.expm1(2.0 * log_decay))
    carry = jnp.exp(log_decay) * (1.0 - starts)
    fresh = factor * entry * conv_out
    return lax.associative_scan(link, (carry, fresh), axis=0)


def body(
    stream,
    doc_starts,
    gain_first,
    proj_inner,
    proj_gate,
    conv_weight,
    conv_bias,
    gate_recur,
    gate_input,
    bias_recur,
    bias_input,
    decay_param,
    proj_out,
    gain_second,
    mlp_gate,
    mlp_up,
    mlp_down,
    cotangent,
):
    count = stream.shape[0]
    own_width = stream.shape[1]
    inner_width = proj_inner.shape[1]
    ffn_width = mlp_gate.shape[1]
    groups = gate_recur.shape[0]
    lag = conv_weight.shape[0] - 1
    column = lax.axis_index("mp") * own_width
    rows_full = lax.all_gather(stream, "mp", axis=1, tiled=True)
    first_norm, first_back = jax.vjp(norm_rows, rows_full, gain_first)
    first_low = first_norm.astype(jnp.bfloat16)
    inner = matmul(first_low, proj_inner)
    gate_pre = matmul(first_low, proj_gate)
    starts = doc_starts.astype(jnp.float32)[:, None]
    keep = 1.0 - starts
    tail_keep = jnp.concatenate([keep[count - lag + 1 :], jnp.ones((1, 1), jnp.float32)], 0)
    tail_mask = jnp.flip(jnp.cumprod(jnp.flip(tail_keep, 0), 0), 0)
    prior = passed_along(inner[count - lag :] * tail_mask, "seq", 1)
    ext_inner = jnp.concatenate([prior, inner], 0)
    ext_keep = jnp.concatenate([jnp.ones((lag, 1), jnp.float32), keep], 0)
    valid = jnp.ones((count, 1), jnp.float32)
    valids = []
    conv_out = conv_weight[0] * inner
    for k in range(1, lag + 1):
        valid = valid * ext_keep[lag - k + 1 : lag - k + 1 + count]
        valids.append(valid)
        conv_out = conv_out + conv_weight[k] * ext_inner[lag - k : lag - k + count] * valid
    conv_out = conv_out + conv_bias
    conv_low = conv_out.astype(jnp.bfloat16)
    recur_pre = block_apply(conv_low, gate_recur) + bias_recur
    input_pre = block_apply(conv_low, gate_input) + bias_input
    scan_fn = partial(local_scan, starts)
    (span, partial_state), scan_back = jax.vjp(scan_fn, conv_out, recur_pre, input_pre, decay_param)
    identity = (jnp.ones((inner_width,), jnp.float32), jnp.zeros((inner_width,), jnp.float32))
    entering = carried_in(
        (span[count - 1], partial_state[count - 1]), "seq", link, identity, False
    )[1]
    states = span * entering + partial_state
    gated, gelu_back = jax.vjp(jax.nn.gelu, gate_pre)
    mixed_low = (gated * states).astype(jnp.bfloat16)
    branch = lax.psum(matmul(mixed_low, proj_out), "mp")
    resid = rows_full + branch
    second_norm, second_back = jax.vjp(norm_rows, resid, gain_second)
    second_low = second_norm.astype(jnp.bfloat16)
    ffn_gate = matmul(second_low, mlp_gate)
    ffn_up = matmul(second_low, mlp_up)
    ffn_act, act_back = jax.vjp(jax.nn.gelu, ffn_gate)
    hidden_low = (ffn_act * ffn_up).astype(jnp.bfloat16)
    mlp_own = lax.psum_scatter(matmul(hidden_low, mlp_down), "mp", scatter_dimension=1, tiled=True)
    output = lax.dynamic_slice_in_dim(resid, column, own_width, 1) + mlp_own
    cot_full = lax.all_gather(cotangent, "mp", axis=1, tiled=True)
    cot_low = cot_full.astype(jnp.bfloat16)
    d_hidden = matmul_nt(cot_low, mlp_down)
    d_gate_ffn = act_back(d_hidden * ffn_up)[0]
    d_pair_low = jnp.concatenate([d_gate_ffn, d_hidden * ffn_act], 1).astype(jnp.bfloat16)
    d_second_part = matmul_nt(d_pair_low[:, :ffn_width], mlp_gate) + matmul_nt(
        d_pair_low[:, ffn_width:], mlp_up
    )
    d_second = lax.psum(d_second_part, "mp")
    d_resid_norm, d_gain_second = second_back(d_second)
    d_resid = cot_full + d_resid_norm
    branch_low = d_resid.astype(jnp.bfloat16)
    d_mixed = matmul_nt(branch_low, proj_out)
    d_states = d_mixed * gated
    d_gate_low = gelu_back(d_mixed * states)[0].astype(jnp.bfloat16)
    outgoing = jnp.sum(d_states * span, axis=0)
    incoming = carried_in((span[count - 1], outgoing), "seq", link, identity, True)[1]
    d_total = d_states.at[count - 1].add(incoming)
    d_conv_direct, d_recur, d_input, d_decay = scan_back((d_total * entering, d_total))
    d_recur_low = d_recur.astype(jnp.bfloat16)
    d_input_low = d_input.astype(jnp.bfloat16)
    d_conv = (
        d_conv_direct + block_back(d_recur_low, gate_recur) + block_back(d_input_low, gate_input)
    )
    grad_gate_recur = block_grad(conv_low, d_recur_low, groups)
    grad_gate_input = block_grad(conv_low, d_input_low, groups)
    grad_bias_recur = jnp.sum(d_recur_low.astype(jnp.float32), axis=0)
    grad_bias_input = jnp.sum(d_input_low.astype(jnp.float32), axis=0)
    ext_grad = (
        jnp.zeros((count + lag, inner_width), jnp.float32).at[lag:].add(conv_weight[0] * d_conv)
    )
    conv_terms = [jnp.sum(d_conv * inner, axis=0)]
    for k in range(1, lag + 1):
        weighted = d_conv * valids[k - 1]
        ext_grad = ext_grad.at[lag - k : lag - k + count].add(conv_weight[k] * weighted)
        conv_terms.append(jnp.sum(weighted * ext_inner[lag - k : lag - k + count], axis=0))
    grad_conv_weight = jnp.stack(conv_terms, 0)
    grad_conv_bias = jnp.sum(d_conv, axis=0)
    returned = passed_along(ext_grad[:lag], "seq", -1)
    d_inner = ext_grad[lag:].at[count - lag :].add(returned * tail_mask)
    d_inner_low = d_inner.astype(jnp.bfloat16)
    first_pair_low = jnp.concatenate([d_inner_low, d_gate_low], 1)
    d_first_part = matmul_nt(d_inner_low, proj_inner) + matmul_nt(d_gate_low, proj_gate)
    d_first = lax.psum(d_first_part, "mp")
    d_rows_norm, d_gain_first = first_back(d_first)
    grad_stream = lax.dynamic_slice_in_dim(d_resid + d_rows_norm, column, own_width, 1)
    small = lax.psum(
        (
            d_gain_first,
            d_gain_second,
            grad_conv_weight,
            grad_conv_bias,
            grad_gate_recur,
            grad_gate_input,
            grad_bias_recur,
            grad_bias_input,
            d_decay,
        ),
        "seq",
    )
    grad_first, grad_out, grad_pair, grad_down = (
        lax.psum_scatter(
            matmul_tn(first_low, first_pair_low), "seq", scatter_dimension=0, tiled=True
        ),
        lax.psum_scatter(matmul_tn(mixed_low, branch_low), "seq", scatter_dimension=0, tiled=True),
        lax.psum_scatter(matmul_tn(second_low, d_pair_low), "seq", scatter_dimension=0, tiled=True),
        lax.psum_scatter(matmul_tn(hidden_low, cot_low), "seq", scatter_dimension=0, tiled=True),
    )
    return (
        output,
        grad_stream,
        small[0],
        grad_first[:, :inner_width],
        grad_first[:, inner_width:],
        small[2],
        small[3],
        small[4],
        small[5],
        small[6],
        small[7],
        small[8],
        grad_out,
        small[1],
        grad_pair[:, :ffn_width],
        grad_pair[:, ffn_width:],
        grad_down,
    )


def solution(mesh):
    in_specs = (
        P("seq", "mp"),
        P("seq"),
        P(),
        P(None, "mp"),
        P(None, "mp"),
        P(None, "mp"),
        P("mp"),
        P("mp", None, None),
        P("mp", None, None),
        P("mp"),
        P("mp"),
        P("mp"),
        P("mp", None),
        P(),
        P(None, "mp"),
        P(None, "mp"),
        P("mp", None),
        P("seq", "mp"),
    )
    out_specs = (
        P("seq", "mp"),
        P("seq", "mp"),
        P(),
        P("seq", "mp"),
        P("seq", "mp"),
        P(None, "mp"),
        P("mp"),
        P("mp", None, None),
        P("mp", None, None),
        P("mp"),
        P("mp"),
        P("mp"),
        P(("mp", "seq"), None),
        P(),
        P("seq", "mp"),
        P("seq", "mp"),
        P(("mp", "seq"), None),
    )
    return jax.shard_map(body, mesh=mesh, in_specs=in_specs, out_specs=out_specs, check_vma=False)
```

profile of v0, /device:TPU:0, one launch (start us, length us, event | category | flops | bytes accessed | tf_op | source)
XLA Modules:
  0.0 1586.7 jit_solution(3280703168751612168)
XLA Ops:
  10.0 83.1 %all-gather.7.cloned.1.call-done = f32[512,2048]{1,0:T(8,128)} async-done(((f32[512,512]{1,0:T(8,128)}), f32[512,2048]{1,0:T(8,128)}) %all-gather.7.cloned.1.call-update) | async-done | bytes 4194320 | tf_op jit(solution)/shard_map/all_gather | solution.py:121
  103.9 5.4 fusion.68
  121.4 4.7 exponential_multiply_fusion
  127.2 3.1 slice.594
  130.3 4.5 slice.593
  134.8 4.3 slice.592
  139.8 4.2 slice.635
  144.1 4.3 slice.675
  148.3 4.2 slice.636
  219.0 4.8 pad.543
  226.0 4.8 pad.561
  234.6 4.8 pad.560
  240.2 12.3 all-gather.2
  255.1 4.8 pad.542
  260.7 8.2 all-gather.1
  269.5 5.7 while.34
  275.2 7.2 multiply_convert_fusion.4
  283.2 3.8 fusion.113
  287.9 152.0 %all-reduce.129.cloned.1.call-done = f32[512,2048]{1,0:T(8,128)} async-done(((f32[512,2048]{1,0:T(8,128)}), f32[512,2048]{1,0:T(8,128)}) %all-reduce.129.cloned.1.call-update) | async-done | bytes 4194320 | tf_op jit(solution)/shard_map/psum | solution.py:153
  439.9 4.0 multiply_reduce_fusion.4
  446.0 10.0 fusion.115
  456.0 5.1 fusion.114
  461.1 60.2 %all-gather.9.cloned.1.call-done = f32[512,2048]{1,0:T(8,128)} async-done(((f32[512,512]{1,0:T(8,128)}), f32[512,2048]{1,0:T(8,128)}) %all-gather.9.cloned.1.call-update) | async-done | bytes 4194320 | tf_op jit(solution)/shard_map/all_gather | solution.py:163
  521.3 12.5 multiply_convert_fusion.2
  533.8 6.7 fusion.117
  540.6 7.9 convolution_add_fusion.1
  551.2 9.5 fusion.116
  560.8 141.4 %all-reduce.131.cloned.1.call-done = f32[512,2048]{1,0:T(8,128)} async-done(((f32[512,2048]{1,0:T(8,128)}), f32[512,2048]{1,0:T(8,128)}) %all-reduce.131.cloned.1.call-update) | async-done | bytes 4194320 | tf_op jit(solution)/shard_map/psum | solution.py:171
  702.2 5.2 multiply_reduce_fusion
  708.1 4.1 fusion
  712.3 7.2 multiply_reduce_fusion.11
  719.5 9.0 all-gather.3
  732.1 5.7 while.35
  744.1 4.2 slice.680
  748.3 3.5 fusion.72
  751.9 4.2 slice.696
  756.1 3.7 fusion.73
  759.8 4.3 slice.681
  764.1 4.2 slice.697
  872.6 3.8 multiply_add_fusion.4
  876.4 4.9 pad.680
  886.7 5.1 pad.621
  891.7 4.9 pad.681
  899.8 5.8 multiply_reduce_fusion.6
  922.2 6.3 multiply_reduce_fusion.9
  931.5 4.4 scatter-add.24
  938.9 4.4 scatter-add.25
  943.3 3.1 constant_dynamic-update-slice_fusion
  947.7 3.9 fusion.118
  952.4 6.8 convolution_add_fusion
  959.3 8.6 fusion.25
  968.0 14.3 fusion.8
  988.0 6.0 fusion.30
  994.1 10.6 fusion.34
  1007.6 106.2 %all-reduce.133.cloned.1.call-done = f32[512,2048]{1,0:T(8,128)} async-done(((f32[512,2048]{1,0:T(8,128)}), f32[512,2048]{1,0:T(8,128)}) %all-reduce.133.cloned.1.call-update) | async-done | bytes 4194320 | tf_op jit(solution)/shard_map/psum | solution.py:206
  1113.8 6.4 multiply_reduce_fusion.1
  1120.2 25.1 %all-reduce.122 = (f32[2048]{0:T(1024)}, f32[4,640]{1,0:T(4,128)}, f32[640]{0:T(1024)}, f32[640]{0:T(1024)}, f32[640]{0:T(1024)}, /*index=5*/f32[640]{0:T(1024)}, f32[2048]{0:T(1024)}) all-reduce(f32[2048]{0:T(1024)S(1)} %get-tuple-element.317, f32[4,640]{1,0:T(4,128)S(1)} %pad_maximum_fusion.15, ...), channel_id=1, replica_groups=mesh['seq'=8,'mp'=4] {'seq'}, use_global_device_ids=true, to_apply=%region_15.16 | all-reduce | flops 9216 | bytes 73728 | tf_op jit(solution)/shard_map/psum | solution.py:209
  1145.3 3.1 fusion.29
  1148.4 49.5 %reduce-scatter.8.cloned.1.call-done = f32[256,1280]{1,0:T(8,128)} async-done(((f32[2048,1280]{1,0:T(8,128)}), f32[256,1280]{1,0:T(8,128)}) %reduce-scatter.8.cloned.1.call-update) | async-done | bytes 1310736 | tf_op jit(solution)/shard_map/reduce_scatter | solution.py:224
  1200.3 158.1 %reduce-scatter.12.cloned.1.call-done = f32[256,3072]{1,0:T(8,128)} async-done(((f32[2048,3072]{1,0:T(8,128)}), f32[256,3072]{1,0:T(8,128)}) %reduce-scatter.12.cloned.1.call-update) | async-done | bytes 3145744 | tf_op jit(solution)/shard_map/reduce_scatter | solution.py:228
  1358.4 3.7 fusion.69
  1362.1 58.5 %all-reduce.135.cloned.1.call-done = (f32[4,160,160]{2,1,0:T(8,128)}, f32[4,160,160]{2,1,0:T(8,128)}) async-done(((f32[4,160,160]{2,1,0:T(8,128)}, f32[4,160,160]{2,1,0:T(8,128)}), (f32[4,160,160]{2,1,0:T(8,128)}, f32[4,160,160]{2,1,0:T(8,128)})) %all-reduce.135.cloned.1.call-update) | async-done | bytes 819216 | tf_op jit(solution)/shard_map/psum | solution.py:209
  1420.6 60.0 %reduce-scatter.10.cloned.1.call-done = f32[80,2048]{1,0:T(8,128)} async-done(((f32[640,2048]{1,0:T(8,128)}), f32[80,2048]{1,0:T(8,128)}) %reduce-scatter.10.cloned.1.call-update) | async-done | bytes 655376 | tf_op jit(solution)/shard_map/reduce_scatter | solution.py:227
  1480.6 96.5 %reduce-scatter.14.cloned.1.call-done = f32[192,2048]{1,0:T(8,128)} async-done(((f32[1536,2048]{1,0:T(8,128)}), f32[192,2048]{1,0:T(8,128)}) %reduce-scatter.14.cloned.1.call-update) | async-done | bytes 1572880 | tf_op jit(solution)/shard_map/reduce_scatter | solution.py:229
  (778 shorter events, 281.8 us)
Async XLA Ops:
  7.2 268.0 %copy-start = (bf16[2048,640]{1,0:T(8,128)(2,1)S(1)}, bf16[2048,640]{1,0:T(8,128)(2,1)}, u32[]{:S(2)}) copy-start(bf16[2048,640]{1,0:T(8,128)(2,1)} %param.38) | copy-start | bytes 7864324
  7.2 85.9 %all-gather.7.cloned.1.call-start = ((), (), s32[]{:S(2)}) async-start(), calls=%async_computation.5 | async-start | bytes 5242880 | tf_op jit(solution)/shard_map/all_gather | solution.py:121
  7.9 431.9 %all-reduce.129.cloned.1.call-start = ((), (), s32[]{:S(2)}) async-start(), calls=%async_computation.6 | async-start | bytes 8388608 | tf_op jit(solution)/shard_map/psum | solution.py:153
  8.7 112.7 %copy-start.115 = (f32[512]{0:T(512)}, f32[512]{0:T(512)S(1)}, u32[]{:S(2)}) copy-start(f32[512]{0:T(512)S(1)} %broadcast_subtract_fusion) | copy-start | bytes 6148
  9.2 90.9 %copy-start.180 = (f32[3,1]{0,1:T(1,128)}, f32[3,1]{0,1:T(1,128)S(1)}, u32[]{:S(2)}) copy-start(f32[3,1]{0,1:T(1,128)S(1)} %rev.14) | copy-start | bytes 40
  9.3 94.6 %copy-start.160 = (f32[512,1]{0,1:T(1,128)}, f32[512,1]{0,1:T(1,128)S(1)}, u32[]{:S(2)}) copy-start(f32[512,1]{0,1:T(1,128)S(1)} %get-tuple-element.399) | copy-start | bytes 6148
  9.3 94.6 %copy-start.162 = (f32[512,1]{0,1:T(1,128)}, f32[512,1]{0,1:T(1,128)S(1)}, u32[]{:S(2)}) copy-start(f32[512,1]{0,1:T(1,128)S(1)} %get-tuple-element.400) | copy-start | bytes 6148
  9.3 86.5 %copy-start.164 = (f32[2048]{0:T(1024)S(1)}, f32[2048]{0:T(1024)}, u32[]{:S(2)}) copy-start(f32[2048]{0:T(1024)} %param.36) | copy-start | bytes 24580
  10.0 111.4 %copy-start.117 = (f32[640]{0:T(1024)}, f32[640]{0:T(1024)S(1)}, u32[]{:S(2)}) copy-start(f32[640]{0:T(1024)S(1)} %broadcast_multiply_fusion.3) | copy-start | bytes 7684
  101.3 2.6 collective-permute-start
  103.6 17.7 %copy-start.166 = (f32[512]{0:T(512)}, f32[512]{0:T(512)S(1)}, u32[]{:S(2)}) copy-start(f32[512]{0:T(512)S(1)} %convert_element_type.44) | copy-start | bytes 6148
  130.3 22.3 %copy-start.17 = (f32[256,640]{1,0:T(8,128)}, f32[256,640]{1,0:T(8,128)S(1)}, u32[]{:S(2)}) copy-start(f32[256,640]{1,0:T(8,128)S(1)} %slice.594) | copy-start | bytes 1966084
  155.0 9.3 copy-start.28
  176.7 8.4 copy-start.61
  185.1 8.0 copy-start.39
  186.5 8.4 copy-start.41
  189.9 9.7 copy-start.22
  275.2 8.1 copy-start.182
  287.1 234.3 %all-gather.9.cloned.1.call-start = ((), (), s32[]{:S(2)}) async-start(), calls=%async_computation.8 | async-start | bytes 5242880 | tf_op jit(solution)/shard_map/all_gather | solution.py:163
  287.8 156.1 %copy-start.129 = (f32[2048]{0:T(1024)S(1)}, f32[2048]{0:T(1024)}, u32[]{:S(2)}) copy-start(f32[2048]{0:T(1024)} %param.47) | copy-start | bytes 24580
  287.8 414.3 %all-reduce.131.cloned.1.call-start = ((), (), s32[]{:S(2)}) async-start(), calls=%async_computation.9 | async-start | bytes 8388608 | tf_op jit(solution)/shard_map/psum | solution.py:171
  443.9 12.1 slice-start.14
  446.0 10.0 copy-start.46
  446.0 10.0 slice-start.15
  548.5 456.3 %reduce-scatter.6.cloned.1.call-start = ((), (), s32[]{:S(2)}) async-start(), calls=%async_computation.7 | async-start | bytes 5242880 | tf_op jit(solution)/shard_map/reduce_scatter | solution.py:161
  560.7 141.5 %copy-start.170 = (f32[512]{0:T(512)S(1)}, f32[512]{0:T(512)}, u32[]{:S(2)}) copy-start(f32[512]{0:T(512)} %copy-done.169) | copy-start | bytes 6148
  560.7 553.0 %all-reduce.133.cloned.1.call-start = ((), (), s32[]{:S(2)}) async-start(), calls=%async_computation.10 | async-start | bytes 8388608 | tf_op jit(solution)/shard_map/psum | solution.py:206
  759.8 8.6 copy-start.38
  799.5 8.9 copy-start.95
  799.5 8.9 copy-start.97
  801.1 8.8 copy-start.109
  803.3 14.4 copy-start.36
  804.9 11.1 copy-start.114
  807.5 10.2 copy-start.119
  808.4 9.4 copy-start.120
  809.8 8.0 copy-start.135
  817.8 7.5 copy-start.93
  825.3 7.8 copy-start.66
  825.3 7.8 copy-start.68
  825.3 7.8 slice-start.8
  825.3 7.8 slice-start.9
  827.1 11.4 copy-start.64
  829.7 12.3 copy-start.92
  831.0 12.4 copy-start.49
  831.0 12.4 copy-start.51
  831.0 12.4 slice-start.6
  831.0 12.4 slice-start.7
  845.5 9.5 copy-start.70
  847.0 9.5 copy-start.33
  847.0 9.5 slice-start.4
  847.0 9.5 slice-start.5
  865.4 7.2 slice-start.2
  865.4 7.2 slice-start.3
  946.4 5.3 collective-permute-start.1
  959.3 238.6 %reduce-scatter.8.cloned.1.call-start = ((), (), s32[]{:S(2)}) async-start(), calls=%async_computation.11 | async-start | bytes 11796480 | tf_op jit(solution)/shard_map/reduce_scatter | solution.py:224
  967.9 390.5 %reduce-scatter.12.cloned.1.call-start = ((), (), s32[]{:S(2)}) async-start(), calls=%async_computation.13 | async-start | bytes 28311552 | tf_op jit(solution)/shard_map/reduce_scatter | solution.py:228
  982.3 438.3 %all-reduce.135.cloned.1.call-start = ((), (), s32[]{:S(2)}) async-start(), calls=%async_computation.15 | async-start | bytes 2621440 | tf_op jit(solution)/shard_map/psum | solution.py:209
  986.9 493.7 %reduce-scatter.10.cloned.1.call-start = ((), (), s32[]{:S(2)}) async-start(), calls=%async_computation.12 | async-start | bytes 5898240 | tf_op jit(solution)/shard_map/reduce_scatter | solution.py:227
  994.1 583.0 %reduce-scatter.14.cloned.1.call-start = ((), (), s32[]{:S(2)}) async-start(), calls=%async_computation.14 | async-start | bytes 14155776 | tf_op jit(solution)/shard_map/reduce_scatter | solution.py:229
  1004.8 108.9 %copy-start.159 = (f32[512]{0:T(512)S(1)}, f32[512]{0:T(512)}, u32[]{:S(2)}) copy-start(f32[512]{0:T(512)} %copy-done.158) | copy-start | bytes 6148
  1004.8 108.9 %copy-start.165 = (f32[2048]{0:T(1024)S(1)}, f32[2048]{0:T(1024)}, u32[]{:S(2)}) copy-start(f32[2048]{0:T(1024)} %param.36) | copy-start | bytes 24580
  1007.6 112.6 %copy-start.168 = (f32[2048]{0:T(1024)S(1)}, f32[2048]{0:T(1024)}, u32[]{:S(2)}) copy-start(f32[2048]{0:T(1024)} %get-tuple-element.315) | copy-start | bytes 24580
  1007.6 137.7 %copy-start.173 = (f32[512]{0:T(512)S(1)}, f32[512]{0:T(512)}, u32[]{:S(2)}) copy-start(f32[512]{0:T(512)} %copy-done.172) | copy-start | bytes 6148
  1420.6 158.5 %copy-start.72 = (f32[4,160,160]{2,1,0:T(8,128)S(1)}, f32[4,160,160]{2,1,0:T(8,128)}, u32[]{:S(2)}) copy-start(f32[4,160,160]{2,1,0:T(8,128)} %get-tuple-element.666) | copy-start | bytes 1228804
  (151 other events, 537.6 us)
Sparse Core Ops, SparseCore 0:
  9.6 83.4 all-gather.6
  287.2 152.6 all-reduce.128
  441.5 79.7 all-gather.8
  548.6 153.4 all-reduce.130
  704.3 75.7 reduce-scatter.5
  959.4 154.2 all-reduce.132
  1117.2 80.5 reduce-scatter.7
  1201.5 156.8 reduce-scatter.11
  1362.8 57.8 all-reduce.134
  1424.8 55.7 reduce-scatter.9
  1484.7 92.3 reduce-scatter.13
where the time goes:
time: 1600 us; the launch traced here: 1590 us
  waiting for transfers between devices  967 us (60%)
  local copies, waits for them, and re-layouts  262 us (16%)
  other arithmetic  146 us (9%)
  matrix products  136 us (8%)
  blocking collectives  54.6 us (3%)
  between operations  16.9 us (1%)
    reduce_scatter x1, waiting for transfers between devices, body(): lax.psum_scatter(matmul_tn(second_low, d_pair_low), 'seq', scatter_dimens...  158 us
    psum x1, waiting for transfers between devices, body(): branch = lax.psum(matmul(mixed_low, proj_out), 'mp')  152 us
    psum x1, waiting for transfers between devices, body(): d_second = lax.psum(d_second_part, 'mp')  141 us
    pad x94, local copies, waits for them, and re-layouts, local_scan(): return lax.associative_scan(link, (carry, fresh), axis=0)  112 us
    psum x1, waiting for transfers between devices, body(): d_first = lax.psum(d_first_part, 'mp')  106 us
    reduce_scatter x1, waiting for transfers between devices, body(): lax.psum_scatter(matmul_tn(hidden_low, cot_low), 'seq', scatter_dimension...  96.5 us
    all_gather x1, waiting for transfers between devices, body(): rows_full = lax.all_gather(stream, 'mp', axis=1, tiled=True)  83.1 us
    slice x92, local copies, waits for them, and re-layouts, local_scan(): return lax.associative_scan(link, (carry, fresh), axis=0)  81.5 us
  transfers between devices with their start and end apart: 13, of which 11 were waited for; matrix products, arithmetic and copies ran while one was open for 21% of the time, Pallas kernels for 0%

commit v1 on v0

--- a/solution.py
+++ b/solution.py
@@ -168,7 +168,9 @@
     d_second_part = matmul_nt(d_pair_low[:, :ffn_width], mlp_gate) + matmul_nt(
         d_pair_low[:, ffn_width:], mlp_up
     )
-    d_second = lax.psum(d_second_part, "mp")
+    d_second = d_second_part
+    for hop in (1, 2):
+        d_second = d_second + lax.ppermute(d_second, "mp", [(dev, dev ^ hop) for dev in range(4)])
     d_resid_norm, d_gain_second = second_back(d_second)
     d_resid = cot_full + d_resid_norm
     branch_low = d_resid.astype(jnp.bfloat16)

time: 1600 us -> 1850 us (1.16)
  waiting for transfers between devices: 967 us -> 1160 us
  local copies, waits for them, and re-layouts: 262 us -> 313 us
    ppermute x0 -> x2, waiting for transfers between devices: none -> 330 us  [body(): lax.ppermute(d_second, 'mp', [(dev, dev ^ hop) for dev in range(4)])]
    psum x1 -> x0, waiting for transfers between devices: 141 us -> none  [body(): d_second = lax.psum(d_second_part, 'mp')]
    slice x92, local copies, waits for them, and re-layouts: 81.5 us -> 136 us  [local_scan(): return lax.associative_scan(link, (carry, fresh), axis=0)]
  transfers between devices with their start and end apart: 13 -> 14, of which waited for: 11 -> 12; matrix products, arithmetic and copies ran while one was open for 21% -> 18% of each run, Pallas kernels for 0% -> 0%
where the time goes in v1:
time: 1850 us; the launch traced here: 1830 us
  waiting for transfers between devices  1160 us (63%)
  local copies, waits for them, and re-layouts  313 us (17%)
  other arithmetic  155 us (8%)
  matrix products  133 us (7%)
  blocking collectives  54.5 us (3%)
    ppermute x2, waiting for transfers between devices, body(): lax.ppermute(d_second, 'mp', [(dev, dev ^ hop) for dev in range(4)])  330 us
    reduce_scatter x1, waiting for transfers between devices, body(): lax.psum_scatter(matmul_tn(second_low, d_pair_low), 'seq', scatter_dimens...  159 us
    psum x1, waiting for transfers between devices, body(): branch = lax.psum(matmul(mixed_low, proj_out), 'mp')  152 us
    slice x92, local copies, waits for them, and re-layouts, local_scan(): return lax.associative_scan(link, (carry, fresh), axis=0)  136 us
    pad x94, local copies, waits for them, and re-layouts, local_scan(): return lax.associative_scan(link, (carry, fresh), axis=0)  111 us
    psum x1, waiting for transfers between devices, body(): d_first = lax.psum(d_first_part, 'mp')  107 us
    reduce_scatter x1, waiting for transfers between devices, body(): lax.psum_scatter(matmul_tn(hidden_low, cot_low), 'seq', scatter_dimension...  96.7 us
    all_gather x1, waiting for transfers between devices, body(): rows_full = lax.all_gather(stream, 'mp', axis=1, tiled=True)  83.1 us
  transfers between devices with their start and end apart: 14, of which 12 were waited for; matrix products, arithmetic and copies ran while one was open for 18% of the time, Pallas kernels for 0%

profile of v1, /device:TPU:0, one launch (start us, length us, event | category | flops | bytes accessed | tf_op | source)
XLA Modules:
  0.0 1834.9 jit_solution(17333081717506756981)
XLA Ops:
  10.0 83.1 %all-gather.7.cloned.1.call-done = f32[512,2048]{1,0:T(8,128)} async-done(((f32[512,512]{1,0:T(8,128)}), f32[512,2048]{1,0:T(8,128)}) %all-gather.7.cloned.1.call-update) | async-done | bytes 4194320 | tf_op jit(solution)/shard_map/all_gather | solution.py:121
  103.9 5.3 fusion.68
  121.4 4.9 exponential_multiply_fusion
  126.3 4.3 slice.592
  130.5 4.2 slice.593
  137.9 4.5 slice.636
  142.4 4.2 slice.635
  235.2 4.3 slice.675
  284.5 4.8 pad.560
  289.3 4.8 pad.561
  294.2 4.8 pad.543
  301.0 4.9 pad.542
  306.6 12.3 all-gather.1
  320.2 8.2 all-gather.2
  329.1 5.7 while.34
  334.8 7.2 multiply_convert_fusion.4
  342.8 3.8 fusion.113
  347.4 152.0 %all-reduce.128.cloned.1.call-done = f32[512,2048]{1,0:T(8,128)} async-done(((f32[512,2048]{1,0:T(8,128)}), f32[512,2048]{1,0:T(8,128)}) %all-reduce.128.cloned.1.call-update) | async-done | bytes 4194320 | tf_op jit(solution)/shard_map/psum | solution.py:153
  499.4 4.0 multiply_reduce_fusion.4
  505.5 10.0 fusion.114
  515.5 5.2 fusion.115
  520.7 60.2 %all-gather.9.cloned.1.call-done = f32[512,2048]{1,0:T(8,128)} async-done(((f32[512,512]{1,0:T(8,128)}), f32[512,2048]{1,0:T(8,128)}) %all-gather.9.cloned.1.call-update) | async-done | bytes 4194320 | tf_op jit(solution)/shard_map/all_gather | solution.py:163
  580.9 12.5 multiply_convert_fusion.2
  593.3 6.7 fusion.117
  600.1 5.7 convolution_add_fusion.1
  605.8 92.3 %collective-permute-done.1 = f32[512,2048]{1,0:T(8,128)S(1)} collective-permute-done((f32[512,2048]{1,0:T(8,128)S(1)}, f32[512,2048]{1,0:T(8,128)S(1)}, u32[]{:S(2)}, u32[]{:S(2)}) %collective-permute-start.1) | collective-permute-done | bytes 4194336 | tf_op jit(solution)/shard_map/ppermute | solution.py:173
  704.5 8.7 fusion.116
  713.3 237.7 %collective-permute-done.2 = f32[512,2048]{1,0:T(8,128)} collective-permute-done((f32[512,2048]{1,0:T(8,128)}, f32[512,2048]{1,0:T(8,128)}, u32[]{:S(2)}, u32[]{:S(2)}) %collective-permute-start.2) | collective-permute-done | bytes 4194336 | tf_op jit(solution)/shard_map/ppermute | solution.py:173
  950.9 6.7 multiply_reduce_fusion
  957.7 5.9 fusion
  963.6 7.5 multiply_reduce_fusion.11
  971.1 8.9 all-gather.3
  983.7 13.8 while.35
  999.6 3.6 fusion.71
  1004.4 4.2 slice.681
  1008.6 4.2 slice.680
  1012.8 3.4 fusion.72
  1016.2 4.2 slice.696
  1020.5 3.6 fusion.73
  1030.5 4.2 slice.697
  1115.8 3.8 multiply_add_fusion.4
  1124.9 4.9 pad.681
  1129.8 4.9 pad.680
  1134.7 3.1 pad.624
  1137.9 4.9 pad.621
  1145.9 5.8 multiply_reduce_fusion.6
  1168.4 6.3 multiply_reduce_fusion.9
  1177.7 4.4 scatter-add.24
  1185.1 4.4 scatter-add.25
  1194.0 3.9 fusion.118
  1198.6 6.8 convolution_add_fusion
  1205.5 8.8 fusion.25
  1214.4 14.3 fusion.8
  1234.4 6.0 fusion.30
  1240.5 10.6 fusion.34
  1254.0 106.6 %all-reduce.130.cloned.1.call-done = f32[512,2048]{1,0:T(8,128)} async-done(((f32[512,2048]{1,0:T(8,128)}), f32[512,2048]{1,0:T(8,128)}) %all-reduce.130.cloned.1.call-update) | async-done | bytes 4194320 | tf_op jit(solution)/shard_map/psum | solution.py:208
  1360.5 6.4 multiply_reduce_fusion.1
  1367.0 25.1 %all-reduce.122 = (f32[2048]{0:T(1024)}, f32[4,640]{1,0:T(4,128)}, f32[640]{0:T(1024)}, f32[640]{0:T(1024)}, f32[640]{0:T(1024)}, /*index=5*/f32[640]{0:T(1024)}, f32[2048]{0:T(1024)}) all-reduce(f32[2048]{0:T(1024)S(1)} %get-tuple-element.317, f32[4,640]{1,0:T(4,128)S(1)} %pad_maximum_fusion.15, ...), channel_id=1, replica_groups=mesh['seq'=8,'mp'=4] {'seq'}, use_global_device_ids=true, to_apply=%region_14.15 | all-reduce | flops 9216 | bytes 73728 | tf_op jit(solution)/shard_map/psum | solution.py:211
  1395.2 49.8 %reduce-scatter.8.cloned.1.call-done = f32[256,1280]{1,0:T(8,128)} async-done(((f32[2048,1280]{1,0:T(8,128)}), f32[256,1280]{1,0:T(8,128)}) %reduce-scatter.8.cloned.1.call-update) | async-done | bytes 1310736 | tf_op jit(solution)/shard_map/reduce_scatter | solution.py:226
  1447.3 158.6 %reduce-scatter.12.cloned.1.call-done = f32[256,3072]{1,0:T(8,128)} async-done(((f32[2048,3072]{1,0:T(8,128)}), f32[256,3072]{1,0:T(8,128)}) %reduce-scatter.12.cloned.1.call-update) | async-done | bytes 3145744 | tf_op jit(solution)/shard_map/reduce_scatter | solution.py:230
  1605.9 3.7 fusion.69
  1609.6 58.9 %all-reduce.132.cloned.1.call-done = (f32[4,160,160]{2,1,0:T(8,128)}, f32[4,160,160]{2,1,0:T(8,128)}) async-done(((f32[4,160,160]{2,1,0:T(8,128)}, f32[4,160,160]{2,1,0:T(8,128)}), (f32[4,160,160]{2,1,0:T(8,128)}, f32[4,160,160]{2,1,0:T(8,128)})) %all-reduce.132.cloned.1.call-update) | async-done | bytes 819216 | tf_op jit(solution)/shard_map/psum | solution.py:211
  1668.5 59.8 %reduce-scatter.10.cloned.1.call-done = f32[80,2048]{1,0:T(8,128)} async-done(((f32[640,2048]{1,0:T(8,128)}), f32[80,2048]{1,0:T(8,128)}) %reduce-scatter.10.cloned.1.call-update) | async-done | bytes 655376 | tf_op jit(solution)/shard_map/reduce_scatter | solution.py:229
  1728.3 96.7 %reduce-scatter.14.cloned.1.call-done = f32[192,2048]{1,0:T(8,128)} async-done(((f32[1536,2048]{1,0:T(8,128)}), f32[192,2048]{1,0:T(8,128)}) %reduce-scatter.14.cloned.1.call-update) | async-done | bytes 1572880 | tf_op jit(solution)/shard_map/reduce_scatter | solution.py:231
  (798 shorter events, 342.0 us)
Async XLA Ops:
  7.2 327.6 %copy-start = (bf16[2048,640]{1,0:T(8,128)(2,1)S(1)}, bf16[2048,640]{1,0:T(8,128)(2,1)}, u32[]{:S(2)}) copy-start(bf16[2048,640]{1,0:T(8,128)(2,1)} %param.38) | copy-start | bytes 7864324
  7.2 85.9 %all-gather.7.cloned.1.call-start = ((), (), s32[]{:S(2)}) async-start(), calls=%async_computation.5 | async-start | bytes 5242880 | tf_op jit(solution)/shard_map/all_gather | solution.py:121
  7.9 491.5 %all-reduce.128.cloned.1.call-start = ((), (), s32[]{:S(2)}) async-start(), calls=%async_computation.6 | async-start | bytes 8388608 | tf_op jit(solution)/shard_map/psum | solution.py:153
  8.7 112.7 %copy-start.115 = (f32[512]{0:T(512)}, f32[512]{0:T(512)S(1)}, u32[]{:S(2)}) copy-start(f32[512]{0:T(512)S(1)} %broadcast_subtract_fusion) | copy-start | bytes 6148
  9.2 90.9 %copy-start.190 = (f32[3,1]{0,1:T(1,128)}, f32[3,1]{0,1:T(1,128)S(1)}, u32[]{:S(2)}) copy-start(f32[3,1]{0,1:T(1,128)S(1)} %rev.14) | copy-start | bytes 40
  9.3 94.6 %copy-start.154 = (f32[512,1]{0,1:T(1,128)}, f32[512,1]{0,1:T(1,128)S(1)}, u32[]{:S(2)}) copy-start(f32[512,1]{0,1:T(1,128)S(1)} %get-tuple-element.399) | copy-start | bytes 6148
  9.3 94.6 %copy-start.156 = (f32[512,1]{0,1:T(1,128)}, f32[512,1]{0,1:T(1,128)S(1)}, u32[]{:S(2)}) copy-start(f32[512,1]{0,1:T(1,128)S(1)} %get-tuple-element.400) | copy-start | bytes 6148
  9.3 86.5 %copy-start.158 = (f32[2048]{0:T(1024)S(1)}, f32[2048]{0:T(1024)}, u32[]{:S(2)}) copy-start(f32[2048]{0:T(1024)} %param.36) | copy-start | bytes 24580
  10.0 111.4 %copy-start.117 = (f32[640]{0:T(1024)}, f32[640]{0:T(1024)S(1)}, u32[]{:S(2)}) copy-start(f32[640]{0:T(1024)S(1)} %broadcast_multiply_fusion.3) | copy-start | bytes 7684
  101.3 2.6 collective-permute-start
  103.7 17.7 copy-start.160
  137.9 8.7 copy-start.19
  163.9 12.5 copy-start.50
  170.0 51.5 %copy-start.67 = (f32[32,640]{1,0:T(8,128)}, f32[32,640]{1,0:T(8,128)S(1)}, u32[]{:S(2)}) copy-start(f32[32,640]{1,0:T(8,128)S(1)} %slice.605) | copy-start | bytes 245764
  176.3 45.2 %copy-start.63 = (f32[64,640]{1,0:T(8,128)S(1)}, f32[64,640]{1,0:T(8,128)}, u32[]{:S(2)}) copy-start(f32[64,640]{1,0:T(8,128)} %get-tuple-element.462) | copy-start | bytes 491524
  187.5 45.0 %copy-start.100 = (f32[8,640]{1,0:T(8,128)}, f32[8,640]{1,0:T(8,128)S(1)}, u32[]{:S(2)}) copy-start(f32[8,640]{1,0:T(8,128)S(1)} %slice.614) | copy-start | bytes 61444
  200.4 39.0 %copy-start.122 = (f32[2,640]{1,0:T(2,128)}, f32[2,640]{1,0:T(2,128)S(1)}, u32[]{:S(2)}) copy-start(f32[2,640]{1,0:T(2,128)S(1)} %slice.621) | copy-start | bytes 15364
  228.4 14.3 copy-start.168
  228.4 14.3 copy-start.179
  228.4 14.3 copy-start.180
  228.4 14.4 copy-start.181
  228.4 14.4 copy-start.182
  228.4 14.4 copy-start.167
  228.4 14.5 copy-start.119
  228.4 14.5 copy-start.143
  231.1 13.4 copy-start.98
  231.1 13.4 copy-start.121
  233.8 12.2 copy-start.85
  233.9 12.2 copy-start.106
  334.8 8.0 copy-start.193
  346.6 234.2 %all-gather.9.cloned.1.call-start = ((), (), s32[]{:S(2)}) async-start(), calls=%async_computation.8 | async-start | bytes 5242880 | tf_op jit(solution)/shard_map/all_gather | solution.py:163
  347.3 156.1 %copy-start.124 = (f32[2048]{0:T(1024)S(1)}, f32[2048]{0:T(1024)}, u32[]{:S(2)}) copy-start(f32[2048]{0:T(1024)} %param.47) | copy-start | bytes 24580
  347.4 903.8 %reduce-scatter.6.cloned.1.call-start = ((), (), s32[]{:S(2)}) async-start(), calls=%async_computation.7 | async-start | bytes 5242880 | tf_op jit(solution)/shard_map/reduce_scatter | solution.py:161
  503.4 12.1 slice-start.10
  505.5 10.0 copy-start.46
  505.5 10.0 slice-start.11
  605.7 92.4 %collective-permute-start.1 = (f32[512,2048]{1,0:T(8,128)S(1)}, f32[512,2048]{1,0:T(8,128)S(1)}, u32[]{:S(2)}, u32[]{:S(2)}) collective-permute-start(f32[512,2048]{1,0:T(8,128)S(1)} %convolution_add_fusion.1), channel_id=1, source_target_pairs={{0,1},{1,0},{2,3},{3,2},{4,5},{5,4},{6,7},{7,6},{8,9},{9,8},{10,11... | collective-permute-start | bytes 12582920 | tf_op jit(solution)/shard_map/ppermute | solution.py:173
  701.0 250.0 %collective-permute-start.2 = (f32[512,2048]{1,0:T(8,128)}, f32[512,2048]{1,0:T(8,128)}, u32[]{:S(2)}, u32[]{:S(2)}) collective-permute-start(f32[512,2048]{1,0:T(8,128)} %add.661), channel_id=1, source_target_pairs={{0,2},{1,3},{2,0},{3,1},{4,6},{5,7},{6,4},{7,5},{8,10},{9,11},{10,... | collective-permute-start | bytes 12582920 | tf_op jit(solution)/shard_map/ppermute | solution.py:173
  713.2 647.3 %all-reduce.130.cloned.1.call-start = ((), (), s32[]{:S(2)}) async-start(), calls=%async_computation.9 | async-start | bytes 8388608 | tf_op jit(solution)/shard_map/psum | solution.py:208
  713.2 244.4 %copy-start.172 = (f32[512]{0:T(512)S(1)}, f32[512]{0:T(512)}, u32[]{:S(2)}) copy-start(f32[512]{0:T(512)} %copy-done.171) | copy-start | bytes 6148
  713.3 244.4 %copy-start.164 = (f32[512]{0:T(512)S(1)}, f32[512]{0:T(512)}, u32[]{:S(2)}) copy-start(f32[512]{0:T(512)} %copy-done.163) | copy-start | bytes 6148
  963.6 7.5 copy-start.7
  1025.2 9.5 copy-start.37
  1071.5 10.0 copy-start.91
  1071.6 11.4 copy-start.51
  1071.6 11.4 copy-start.52
  1071.6 11.4 slice-start.6
  1071.6 11.4 slice-start.7
  1085.0 8.1 copy-start.72
  1086.5 9.6 copy-start.71
  1088.2 9.4 copy-start.33
  1088.2 9.4 slice-start.4
  1088.2 9.4 slice-start.5
  1192.6 5.3 collective-permute-start.3
  1205.4 239.5 %reduce-scatter.8.cloned.1.call-start = ((), (), s32[]{:S(2)}) async-start(), calls=%async_computation.10 | async-start | bytes 11796480 | tf_op jit(solution)/shard_map/reduce_scatter | solution.py:226
  1214.3 391.6 %reduce-scatter.12.cloned.1.call-start = ((), (), s32[]{:S(2)}) async-start(), calls=%async_computation.12 | async-start | bytes 28311552 | tf_op jit(solution)/shard_map/reduce_scatter | solution.py:230
  1228.7 439.8 %all-reduce.132.cloned.1.call-start = ((), (), s32[]{:S(2)}) async-start(), calls=%async_computation.14 | async-start | bytes 2621440 | tf_op jit(solution)/shard_map/psum | solution.py:211
  1233.3 495.0 %reduce-scatter.10.cloned.1.call-start = ((), (), s32[]{:S(2)}) async-start(), calls=%async_computation.11 | async-start | bytes 5898240 | tf_op jit(solution)/shard_map/reduce_scatter | solution.py:229
  1240.4 584.6 %reduce-scatter.14.cloned.1.call-start = ((), (), s32[]{:S(2)}) async-start(), calls=%async_computation.13 | async-start | bytes 14155776 | tf_op jit(solution)/shard_map/reduce_scatter | solution.py:231
  1251.1 109.5 %copy-start.153 = (f32[512]{0:T(512)S(1)}, f32[512]{0:T(512)}, u32[]{:S(2)}) copy-start(f32[512]{0:T(512)} %copy-done.152) | copy-start | bytes 6148
  1251.1 109.4 %copy-start.159 = (f32[2048]{0:T(1024)S(1)}, f32[2048]{0:T(1024)}, u32[]{:S(2)}) copy-start(f32[2048]{0:T(1024)} %param.36) | copy-start | bytes 24580
  1253.9 113.0 %copy-start.162 = (f32[2048]{0:T(1024)S(1)}, f32[2048]{0:T(1024)}, u32[]{:S(2)}) copy-start(f32[2048]{0:T(1024)} %get-tuple-element.315) | copy-start | bytes 24580
  1253.9 138.1 %copy-start.170 = (f32[512]{0:T(512)S(1)}, f32[512]{0:T(512)}, u32[]{:S(2)}) copy-start(f32[512]{0:T(512)} %copy-done.169) | copy-start | bytes 6148
  1668.5 158.5 %copy-start.73 = (f32[4,160,160]{2,1,0:T(8,128)S(1)}, f32[4,160,160]{2,1,0:T(8,128)}, u32[]{:S(2)}) copy-start(f32[4,160,160]{2,1,0:T(8,128)} %get-tuple-element.666) | copy-start | bytes 1228804
  (159 other events, 532.0 us)
Sparse Core Ops, SparseCore 0:
  9.6 83.4 all-gather.6
  346.7 152.6 all-reduce.127
  501.0 79.7 all-gather.8
  713.3 167.8 reduce-scatter.5
  1205.5 154.9 all-reduce.129
  1364.3 80.5 reduce-scatter.7
  1449.0 156.8 reduce-scatter.11
  1610.6 57.8 all-reduce.131
  1672.5 55.7 reduce-scatter.9
  1732.6 92.3 reduce-scatter.13
